TPU v7x, 512 devices: a whole 4x8x8 slice. The times are simulated.
512 devices in a mesh: slab: 8 (over z), energy: 64 (over y, x, core).
Axes of the slice: x: 4, y: 8, z: 8, core: 2. Of those that a mesh axis runs over, the one named last changes fastest.
Arguments:
- retarded: float32 [8, 128, 2, 256, 256], P('slab', 'energy'), may hold values from -0.375 to 0.375
- lesser_prev: float32 [8, 128, 2, 256, 256], P('slab', 'energy'), may hold values from -1.8 to 1.8
- hopping: float32 [8, 256, 256], P('slab'), may hold values from -0.375 to 0.375
- hop_mask: int32 [8, 4, 4], P('slab'), may hold values 0 or 1
- offsets: int32 [3], replicated, may hold values from 1 to 6, as said below
- coupling: float32 [3], replicated, may hold values from 0.3 to 1
- occupation: float32 [3], replicated, may hold values from 0.1 to 3
Outputs:
- lesser: float32 [8, 128, 2, 256, 256], P('slab', 'energy')
Inputs may be any that keep to these rules, and one draw needn't show every extreme that they name: `offsets`: the offset of mode k lies in k * 2 + 1 to (k + 1) * 2, and the last mode's equals 6.
All inputs are finite; a program needn't handle non-finite values. No bound on the sum of `hop_mask` on one device may be relied on, other than what follows from the above.
Results may differ from a plain program's by a relative error of at most 0.00014.
Values sent between devices are 32-bit elements; how exact they have to be, the bound alone decides.
A program may use at most 64 MiB of HBM per device.

v0:
```python
import jax
import jax.numpy as jnp
from jax import lax
from jax.sharding import PartitionSpec as P


def from_behind(value, axis, by):
    devices = lax.axis_size(axis)
    pairs = [(i, i + by) for i in range(devices) if 0 <= i + by < devices]
    return lax.ppermute(value, axis, pairs)


def matmul_high(left_matrix, right_matrix):
    return jnp.einsum(
        "...ij,...jk->...ik",
        left_matrix,
        right_matrix,
        precision=lax.Precision.HIGHEST,
        preferred_element_type=jnp.float32,
    )


def matmul_transposed(left_matrix, right_matrix):
    return jnp.einsum(
        "...ij,...kj->...ik",
        left_matrix,
        right_matrix,
        precision=lax.Precision.HIGHEST,
        preferred_element_type=jnp.float32,
    )


def complex_product(left_factor, right_factor):
    left_real, left_imag = (left_factor[..., 0, :, :], left_factor[..., 1, :, :])
    right_real, right_imag = (right_factor[..., 0, :, :], right_factor[..., 1, :, :])
    real_part = matmul_high(left_real, right_real) - matmul_high(left_imag, right_imag)
    imag_part = matmul_high(left_real, right_imag) + matmul_high(left_imag, right_real)
    return jnp.stack([real_part, imag_part], axis=-3)


def product_adjoint(left_factor, right_factor):
    left_real, left_imag = (left_factor[..., 0, :, :], left_factor[..., 1, :, :])
    right_real, right_imag = (right_factor[..., 0, :, :], right_factor[..., 1, :, :])
    real_part = matmul_transposed(left_real, right_real) + matmul_transposed(left_imag, right_imag)
    imag_part = matmul_transposed(left_imag, right_real) - matmul_transposed(left_real, right_imag)
    return jnp.stack([real_part, imag_part], axis=-3)


def masked_hopping(hopping_block, mask_block):
    blocks = mask_block.shape[-1]
    tile_size = hopping_block.shape[-1] // blocks
    expanded = jnp.broadcast_to(
        mask_block.astype(jnp.float32)[:, None, :, None], (blocks, tile_size, blocks, tile_size)
    )
    return hopping_block * expanded.reshape(blocks * tile_size, blocks * tile_size)


def offset_term(piece, distance, offsets, coupling, occupation):
    per_device = piece.shape[1]
    source_energy = jnp.arange(per_device, dtype=jnp.int32)[None, :]
    target_energy = jnp.arange(per_device, dtype=jnp.int32)[:, None]
    delta = distance * per_device + source_energy - target_energy
    emission = (offsets[:, None, None] == delta[None]).astype(jnp.float32)
    absorption = (offsets[:, None, None] == -delta[None]).astype(jnp.float32)
    factors = coupling[:, None, None] * (
        (occupation[:, None, None] + 1.0) * emission + occupation[:, None, None] * absorption
    )
    weights = jnp.sum(factors, axis=0)
    return jnp.einsum(
        "ji,sixyz->sjxyz",
        weights,
        piece,
        precision=lax.Precision.HIGHEST,
        preferred_element_type=jnp.float32,
    )


def body(retarded, lesser_prev, hopping, hop_mask, offsets, coupling, occupation):
    mode_count = offsets.shape[0]
    self_energy = offset_term(lesser_prev, 0, offsets, coupling, occupation)
    for distance in range(1, mode_count + 1):
        upper_piece = from_behind(lesser_prev, "energy", -distance)
        lower_piece = from_behind(lesser_prev, "energy", distance)
        self_energy = self_energy + offset_term(
            upper_piece, distance, offsets, coupling, occupation
        )
        self_energy = self_energy + offset_term(
            lower_piece, -distance, offsets, coupling, occupation
        )
    coupled = matmul_high(retarded, masked_hopping(hopping[0], hop_mask[0]))
    source = product_adjoint(complex_product(retarded, self_energy), retarded)
    position = lax.axis_index("slab")

    def advance(turn_number, current):
        incoming = from_behind(current, "slab", 1)
        return lax.cond(
            position == turn_number,
            lambda: source + product_adjoint(complex_product(coupled, incoming), coupled),
            lambda: current,
        )

    lesser = lax.fori_loop(1, lax.axis_size("slab"), advance, source)
    return lesser


def solution(mesh):
    return jax.shard_map(
        body,
        mesh=mesh,
        in_specs=(
            P("slab", "energy", None, None, None),
            P("slab", "energy", None, None, None),
            P("slab", None, None),
            P("slab", None, None),
            P(),
            P(),
            P(),
        ),
        out_specs=P("slab", "energy", None, None, None),
        check_vma=False,
    )
```

profile of v0, /device:TPU:486, one launch (start us, length us, event | category | flops | bytes accessed | tf_op | source)
XLA Modules:
  0.0 342.7 jit_solution(9665465504394522874)
XLA Ops:
  0.0 3.0 copy.29
  3.0 2.9 collective-permute-start.5
  5.9 4.9 %collective-permute-start.4 = (f32[1,2,2,256,256]{4,1,3,2,0:T(2,128)}, f32[1,2,2,256,256]{4,1,3,2,0:T(2,128)}, u32[]{:S(2)}, u32[]{:S(2)}) collective-permute-start(f32[1,2,2,256,256]{4,1,3,2,0:T(2,128)} %copy.29), channel_id=1, source_target_pairs={{0,2},{1,3},{2,4},{3,5},{4,6},{5,7},{6,8},{7,9},{8,10},{9,11},{10,... | collective-permute-start | bytes 3145736 | tf_op jit(solution)/shard_map/ppermute | solution.py:10
  10.8 1.9 collective-permute-start.3
  12.8 5.5 %collective-permute-start.6 = (f32[1,2,2,256,256]{4,1,3,2,0:T(2,128)}, f32[1,2,2,256,256]{4,1,3,2,0:T(2,128)}, u32[]{:S(2)}, u32[]{:S(2)}) collective-permute-start(f32[1,2,2,256,256]{4,1,3,2,0:T(2,128)} %copy.29), channel_id=1, source_target_pairs={{0,3},{1,4},{2,5},{3,6},{4,7},{5,8},{6,9},{7,10},{8,11},{9,12},{10... | collective-permute-start | bytes 3145736 | tf_op jit(solution)/shard_map/ppermute | solution.py:10
  19.5 1.9 convolution_bitcast_fusion
  22.6 5.5 %fusion.48 = f32[2,2,256,256]{3,0,2,1:T(2,128)S(1)} fusion(f32[2,2,256,256]{3,2,1,0:T(8,128)} %bitcast.148, f32[2,2]{1,0:T(2,128)S(1)} %get-tuple-element.133), kind=kOutput, calls=%fused_computation.61 | convolution fusion | flops 6291456 | bytes 2097168 | tf_op jit(solution)/shard_map/ji,sixyz->sjxyz/dot_general | solution.py:69
  28.1 3.3 collective-permute-start.1
  31.4 2.9 collective-permute-done.5
  34.3 5.0 %fusion.40 = f32[2,2,256,256]{3,0,2,1:T(2,128)S(1)} fusion(f32[1,2,2,256,256]{4,1,3,2,0:T(2,128)} %collective-permute-done.5, f32[2,2]{1,0:T(2,128)S(1)} %get-tuple-element.131), kind=kOutput, calls=%fused_computation.53 | convolution fusion | flops 6291456 | bytes 2097168 | tf_op jit(solution)/shard_map/ji,sixyz->sjxyz/dot_general | solution.py:69
  39.4 1.9 collective-permute-start.2
  41.3 33.7 %collective-permute-done.4 = f32[1,2,2,256,256]{4,1,3,2,0:T(2,128)} collective-permute-done((f32[1,2,2,256,256]{4,1,3,2,0:T(2,128)}, f32[1,2,2,256,256]{4,1,3,2,0:T(2,128)}, u32[]{:S(2)}, u32[]{:S(2)}) %collective-permute-start.4) | collective-permute-done | bytes 1048608 | tf_op jit(solution)/shard_map/ppermute | solution.py:10
  75.0 5.0 %fusion.42 = f32[2,2,256,256]{3,0,2,1:T(2,128)S(1)} fusion(f32[1,2,2,256,256]{4,1,3,2,0:T(2,128)} %collective-permute-done.4, f32[2,2]{1,0:T(2,128)S(1)} %get-tuple-element.130), kind=kOutput, calls=%fused_computation.55 | convolution fusion | flops 6291456 | bytes 2097168 | tf_op jit(solution)/shard_map/ji,sixyz->sjxyz/dot_general | solution.py:69
  80.1 5.0 %fusion.44 = f32[2,2,256,256]{3,0,2,1:T(2,128)S(1)} fusion(f32[1,2,2,256,256]{4,1,3,2,0:T(2,128)} %collective-permute-done.3, f32[2,2]{1,0:T(2,128)S(1)} %get-tuple-element.129), kind=kOutput, calls=%fused_computation.57 | convolution fusion | flops 6291456 | bytes 2097168 | tf_op jit(solution)/shard_map/ji,sixyz->sjxyz/dot_general | solution.py:69
  85.1 5.0 %fusion.38 = f32[2,2,256,256]{3,0,2,1:T(2,128)S(1)} fusion(f32[1,2,2,256,256]{4,1,3,2,0:T(2,128)} %collective-permute-done.6, f32[2,2]{1,0:T(2,128)S(1)} %get-tuple-element.132), kind=kOutput, calls=%fused_computation.51 | convolution fusion | flops 6291456 | bytes 2097168 | tf_op jit(solution)/shard_map/ji,sixyz->sjxyz/dot_general | solution.py:69
  90.1 12.6 %convolution_add_fusion.3 = f32[2,2,256,256]{3,0,2,1:T(2,128)S(1)} fusion(f32[2,2,256,256]{3,0,2,1:T(2,128)S(1)} %fusion.48, f32[1,2,2,256,256]{4,1,3,2,0:T(2,128)S(1)} %collective-permute-done.1, f32[2,2]{1,0:T(2,128)S(1)} %get-tuple-element.128), kind=kOutput, calls=%fused_computation.38 | convolution fusion | flops 6553600 | bytes 3145744 | tf_op jit(solution)/shard_map/ji,sixyz->sjxyz/dot_general | solution.py:69
  102.7 5.1 %fusion.36 = f32[1,2,2,256,256]{4,1,3,2,0:T(2,128)S(1)} fusion(f32[2,2,256,256]{3,0,2,1:T(2,128)S(1)} %fusion.38, f32[2,2,256,256]{3,0,2,1:T(2,128)S(1)} %fusion.40, f32[2,2,256,256]{3,0,2,1:T(2,128)S(1)} %fusion.42, f32[2,2,256,256]{3,0,2,1:T(2,128)S(1)} %fusion.44, f32[2,2,256,256]{3,0,2,1:T(2,128)S(1)} %convolution_add_fusion.3, ...), kind=kOutput, calls=%fused_computation.48 | convolution fusion | flops 7602176 | bytes 7340048 | tf_op jit(solution)/shard_map/ji,sixyz->sjxyz/dot_general | solution.py:69
  109.2 1.5 fusion.60
  119.5 220.7 %while.16 = (s32[]{:T(128)}, f32[1,2,2,256,256]{4,3,1,2,0:T(8,128)}, s32[]{:T(128)}, f32[1,2,2,256,256]{4,3,1,2,0:T(8,128)S(1)}, f32[1,2,2,256,256]{4,3,1,2,0:T(8,128)S(1)}, /*index=5*/s32[]{:T(128)}) while((s32[]{:T(128)}, f32[1,2,2,256,256]{4,3,1,2,0:T(8,128)}, s32[]{:T(128)}, f32[1,2,2,256,256]{4,3,1,2,0:T(8,128)S(1)}, ...), condition=%wide.region_10.0_spmd, body=%wide.region_7.0_spmd.sunk | while | flops 3222274048 | bytes 22020252 | solution.py:102
  119.7 1.3 collective-permute-start
  121.0 23.7 %collective-permute-done = f32[1,2,2,256,256]{4,3,1,2,0:T(8,128)S(1)} collective-permute-done((f32[1,2,2,256,256]{4,3,1,2,0:T(8,128)}, f32[1,2,2,256,256]{4,3,1,2,0:T(8,128)S(1)}, u32[]{:S(2)}, u32[]{:S(2)}) %collective-permute-start) | collective-permute-done | bytes 1048608 | tf_op jit(solution)/shard_map/while/body/eval_jaxpr/ppermute | solution.py:10
  144.8 1.3 collective-permute-start
  146.1 24.9 %collective-permute-done = f32[1,2,2,256,256]{4,3,1,2,0:T(8,128)S(1)} collective-permute-done((f32[1,2,2,256,256]{4,3,1,2,0:T(8,128)}, f32[1,2,2,256,256]{4,3,1,2,0:T(8,128)S(1)}, u32[]{:S(2)}, u32[]{:S(2)}) %collective-permute-start) | collective-permute-done | bytes 1048608 | tf_op jit(solution)/shard_map/while/body/eval_jaxpr/ppermute | solution.py:10
  171.0 1.3 collective-permute-start
  172.2 26.0 %collective-permute-done = f32[1,2,2,256,256]{4,3,1,2,0:T(8,128)S(1)} collective-permute-done((f32[1,2,2,256,256]{4,3,1,2,0:T(8,128)}, f32[1,2,2,256,256]{4,3,1,2,0:T(8,128)S(1)}, u32[]{:S(2)}, u32[]{:S(2)}) %collective-permute-start) | collective-permute-done | bytes 1048608 | tf_op jit(solution)/shard_map/while/body/eval_jaxpr/ppermute | solution.py:10
  199.6 26.5 %collective-permute-done = f32[1,2,2,256,256]{4,3,1,2,0:T(8,128)S(1)} collective-permute-done((f32[1,2,2,256,256]{4,3,1,2,0:T(8,128)}, f32[1,2,2,256,256]{4,3,1,2,0:T(8,128)S(1)}, u32[]{:S(2)}, u32[]{:S(2)}) %collective-permute-start) | collective-permute-done | bytes 1048608 | tf_op jit(solution)/shard_map/while/body/eval_jaxpr/ppermute | solution.py:10
  226.1 1.3 collective-permute-start
  227.4 25.6 %collective-permute-done = f32[1,2,2,256,256]{4,3,1,2,0:T(8,128)S(1)} collective-permute-done((f32[1,2,2,256,256]{4,3,1,2,0:T(8,128)}, f32[1,2,2,256,256]{4,3,1,2,0:T(8,128)S(1)}, u32[]{:S(2)}, u32[]{:S(2)}) %collective-permute-start) | collective-permute-done | bytes 1048608 | tf_op jit(solution)/shard_map/while/body/eval_jaxpr/ppermute | solution.py:10
  254.3 25.7 %collective-permute-done = f32[1,2,2,256,256]{4,3,1,2,0:T(8,128)S(1)} collective-permute-done((f32[1,2,2,256,256]{4,3,1,2,0:T(8,128)}, f32[1,2,2,256,256]{4,3,1,2,0:T(8,128)S(1)}, u32[]{:S(2)}, u32[]{:S(2)}) %collective-permute-start) | collective-permute-done | bytes 1048608 | tf_op jit(solution)/shard_map/while/body/eval_jaxpr/ppermute | solution.py:10
  281.3 52.5 %collective-permute-done = f32[1,2,2,256,256]{4,3,1,2,0:T(8,128)S(1)} collective-permute-done((f32[1,2,2,256,256]{4,3,1,2,0:T(8,128)}, f32[1,2,2,256,256]{4,3,1,2,0:T(8,128)S(1)}, u32[]{:S(2)}, u32[]{:S(2)}) %collective-permute-start) | collective-permute-done | bytes 1048608 | tf_op jit(solution)/shard_map/while/body/eval_jaxpr/ppermute | solution.py:10
  333.8 6.4 %conditional.2 = (f32[1,2,2,256,256]{4,3,1,2,0:T(8,128)}) conditional(s32[]{:T(128)} %convert_element_type.35, f32[1,2,2,256,256]{4,3,1,2,0:T(8,128)} %get-tuple-element.204, (f32[1,2,2,256,256]{4,3,1,2,0:T(8,128)S(1)}, f32[1,2,2,256,256]{4,3,1,2,0:T(8,128)S(1)}, f32[1,2,2,256,256]{4,3,1,2,0:T(8,128)S(1)}) %tuple.61), branch_computations={%region_8.0_spmd, %region_9.0_spmd} | conditional | flops 3222274048 | bytes 17825800 | solution.py:96
  340.2 2.3 copy.47
  (64 shorter events, 22.7 us)
Async XLA Ops:
  0.0 18.3 %copy-start.4 = (f32[3]{0:T(128)S(1)}, f32[3]{0:T(128)}, u32[]{:S(2)}) copy-start(f32[3]{0:T(128)} %param.17) | copy-start | bytes 40
  0.0 18.3 %copy-start.3 = (s32[1,4,4]{2,1,0:T(4,128)S(1)}, s32[1,4,4]{2,1,0:T(4,128)}, u32[]{:S(2)}) copy-start(s32[1,4,4]{2,1,0:T(4,128)} %param.14) | copy-start | bytes 196
  3.0 15.8 %copy-start = (f32[1,2,2,256,256]{4,3,2,1,0:T(8,128)S(1)}, f32[1,2,2,256,256]{4,3,2,1,0:T(8,128)}, u32[]{:S(2)}) copy-start(f32[1,2,2,256,256]{4,3,2,1,0:T(8,128)} %param.11) | copy-start | bytes 3145732
  3.0 31.3 %collective-permute-start.5 = (f32[1,2,2,256,256]{4,1,3,2,0:T(2,128)}, f32[1,2,2,256,256]{4,1,3,2,0:T(2,128)}, u32[]{:S(2)}, u32[]{:S(2)}) collective-permute-start(f32[1,2,2,256,256]{4,1,3,2,0:T(2,128)} %copy.29), channel_id=1, source_target_pairs={{3,0},{4,1},{5,2},{6,3},{7,4},{8,5},{9,6},{10,7},{11,8},{12,9},{13... | collective-permute-start | bytes 3145736 | tf_op jit(solution)/shard_map/ppermute | solution.py:10
  5.9 69.1 %collective-permute-start.4 = (f32[1,2,2,256,256]{4,1,3,2,0:T(2,128)}, f32[1,2,2,256,256]{4,1,3,2,0:T(2,128)}, u32[]{:S(2)}, u32[]{:S(2)}) collective-permute-start(f32[1,2,2,256,256]{4,1,3,2,0:T(2,128)} %copy.29), channel_id=1, source_target_pairs={{0,2},{1,3},{2,4},{3,5},{4,6},{5,7},{6,8},{7,9},{8,10},{9,11},{10,... | collective-permute-start | bytes 3145736 | tf_op jit(solution)/shard_map/ppermute | solution.py:10
  10.8 69.2 %collective-permute-start.3 = (f32[1,2,2,256,256]{4,1,3,2,0:T(2,128)}, f32[1,2,2,256,256]{4,1,3,2,0:T(2,128)}, u32[]{:S(2)}, u32[]{:S(2)}) collective-permute-start(f32[1,2,2,256,256]{4,1,3,2,0:T(2,128)} %copy.29), channel_id=1, source_target_pairs={{2,0},{3,1},{4,2},{5,3},{6,4},{7,5},{8,6},{9,7},{10,8},{11,9},{12,... | collective-permute-start | bytes 3145736 | tf_op jit(solution)/shard_map/ppermute | solution.py:10
  12.8 72.3 %collective-permute-start.6 = (f32[1,2,2,256,256]{4,1,3,2,0:T(2,128)}, f32[1,2,2,256,256]{4,1,3,2,0:T(2,128)}, u32[]{:S(2)}, u32[]{:S(2)}) collective-permute-start(f32[1,2,2,256,256]{4,1,3,2,0:T(2,128)} %copy.29), channel_id=1, source_target_pairs={{0,3},{1,4},{2,5},{3,6},{4,7},{5,8},{6,9},{7,10},{8,11},{9,12},{10... | collective-permute-start | bytes 3145736 | tf_op jit(solution)/shard_map/ppermute | solution.py:10
  18.5 1.0 copy-start.2
  21.7 0.7 copy-start.5
  21.7 0.7 copy-start.6
  28.1 62.0 %collective-permute-start.1 = (f32[1,2,2,256,256]{4,1,3,2,0:T(2,128)}, f32[1,2,2,256,256]{4,1,3,2,0:T(2,128)S(1)}, u32[]{:S(2)}, u32[]{:S(2)}) collective-permute-start(f32[1,2,2,256,256]{4,1,3,2,0:T(2,128)} %copy.29), channel_id=1, source_target_pairs={{1,0},{2,1},{3,2},{4,3},{5,4},{6,5},{7,6},{8,7},{9,8},{10,9},{11,1... | collective-permute-start | bytes 3145736 | tf_op jit(solution)/shard_map/ppermute | solution.py:10
  39.4 63.3 %collective-permute-start.2 = (f32[1,2,2,256,256]{4,1,3,2,0:T(2,128)}, f32[1,2,2,256,256]{4,1,3,2,0:T(2,128)S(1)}, u32[]{:S(2)}, u32[]{:S(2)}) collective-permute-start(f32[1,2,2,256,256]{4,1,3,2,0:T(2,128)} %copy.29), channel_id=1, source_target_pairs={{0,1},{1,2},{2,3},{3,4},{4,5},{5,6},{6,7},{7,8},{8,9},{9,10},{10,1... | collective-permute-start | bytes 3145736 | tf_op jit(solution)/shard_map/ppermute | solution.py:10
  111.9 1.0 copy-start.1
  119.7 25.0 %collective-permute-start = (f32[1,2,2,256,256]{4,3,1,2,0:T(8,128)}, f32[1,2,2,256,256]{4,3,1,2,0:T(8,128)S(1)}, u32[]{:S(2)}, u32[]{:S(2)}) collective-permute-start(f32[1,2,2,256,256]{4,3,1,2,0:T(8,128)} %get-tuple-element.204), channel_id=1, source_target_pairs={{0,64},{64,128},{128,192},{192,256},{256,320},{320,384},{384,448},... | collective-permute-start | bytes 3145736 | tf_op jit(solution)/shard_map/while/body/eval_jaxpr/ppermute | solution.py:10
  144.8 26.2 %collective-permute-start = (f32[1,2,2,256,256]{4,3,1,2,0:T(8,128)}, f32[1,2,2,256,256]{4,3,1,2,0:T(8,128)S(1)}, u32[]{:S(2)}, u32[]{:S(2)}) collective-permute-start(f32[1,2,2,256,256]{4,3,1,2,0:T(8,128)} %get-tuple-element.204), channel_id=1, source_target_pairs={{0,64},{64,128},{128,192},{192,256},{256,320},{320,384},{384,448},... | collective-permute-start | bytes 3145736 | tf_op jit(solution)/shard_map/while/body/eval_jaxpr/ppermute | solution.py:10
  171.0 27.3 %collective-permute-start = (f32[1,2,2,256,256]{4,3,1,2,0:T(8,128)}, f32[1,2,2,256,256]{4,3,1,2,0:T(8,128)S(1)}, u32[]{:S(2)}, u32[]{:S(2)}) collective-permute-start(f32[1,2,2,256,256]{4,3,1,2,0:T(8,128)} %get-tuple-element.204), channel_id=1, source_target_pairs={{0,64},{64,128},{128,192},{192,256},{256,320},{320,384},{384,448},... | collective-permute-start | bytes 3145736 | tf_op jit(solution)/shard_map/while/body/eval_jaxpr/ppermute | solution.py:10
  198.3 27.8 %collective-permute-start = (f32[1,2,2,256,256]{4,3,1,2,0:T(8,128)}, f32[1,2,2,256,256]{4,3,1,2,0:T(8,128)S(1)}, u32[]{:S(2)}, u32[]{:S(2)}) collective-permute-start(f32[1,2,2,256,256]{4,3,1,2,0:T(8,128)} %get-tuple-element.204), channel_id=1, source_target_pairs={{0,64},{64,128},{128,192},{192,256},{256,320},{320,384},{384,448},... | collective-permute-start | bytes 3145736 | tf_op jit(solution)/shard_map/while/body/eval_jaxpr/ppermute | solution.py:10
  226.1 26.9 %collective-permute-start = (f32[1,2,2,256,256]{4,3,1,2,0:T(8,128)}, f32[1,2,2,256,256]{4,3,1,2,0:T(8,128)S(1)}, u32[]{:S(2)}, u32[]{:S(2)}) collective-permute-start(f32[1,2,2,256,256]{4,3,1,2,0:T(8,128)} %get-tuple-element.204), channel_id=1, source_target_pairs={{0,64},{64,128},{128,192},{192,256},{256,320},{320,384},{384,448},... | collective-permute-start | bytes 3145736 | tf_op jit(solution)/shard_map/while/body/eval_jaxpr/ppermute | solution.py:10
  253.0 27.0 %collective-permute-start = (f32[1,2,2,256,256]{4,3,1,2,0:T(8,128)}, f32[1,2,2,256,256]{4,3,1,2,0:T(8,128)S(1)}, u32[]{:S(2)}, u32[]{:S(2)}) collective-permute-start(f32[1,2,2,256,256]{4,3,1,2,0:T(8,128)} %get-tuple-element.204), channel_id=1, source_target_pairs={{0,64},{64,128},{128,192},{192,256},{256,320},{320,384},{384,448},... | collective-permute-start | bytes 3145736 | tf_op jit(solution)/shard_map/while/body/eval_jaxpr/ppermute | solution.py:10
  280.0 53.8 %collective-permute-start = (f32[1,2,2,256,256]{4,3,1,2,0:T(8,128)}, f32[1,2,2,256,256]{4,3,1,2,0:T(8,128)S(1)}, u32[]{:S(2)}, u32[]{:S(2)}) collective-permute-start(f32[1,2,2,256,256]{4,3,1,2,0:T(8,128)} %get-tuple-element.204), channel_id=1, source_target_pairs={{0,64},{64,128},{128,192},{192,256},{256,320},{320,384},{384,448},... | collective-permute-start | bytes 3145736 | tf_op jit(solution)/shard_map/while/body/eval_jaxpr/ppermute | solution.py:10
where the time goes:
time: 346 us; the launch traced here: 343 us
  waiting for transfers between devices  242 us (70%)
  matrix products  58 us (17%)
  starting transfers between devices  29.4 us (8%)
  local copies, waits for them, and re-layouts  11.3 us (3%)
    ppermute x13, waiting for transfers between devices, from_behind(): return lax.ppermute(value, axis, pairs)  242 us
    dot_general x7, matrix products, offset_term(): jnp.einsum('ji,sixyz->sjxyz', weights, piece, precision=lax.Precision.HIG...  43.2 us
    ppermute x13, starting transfers between devices, from_behind(): return lax.ppermute(value, axis, pairs)  29.4 us
    dot_general x9, matrix products, matmul_high(): jnp.einsum('...ij,...jk->...ik', left_matrix, right_matrix, precision=lax...  7.93 us
  transfers between devices with their start and end apart: 13, of which 9 were waited for; matrix products, arithmetic and copies ran while one was open for 12% of the time, Pallas kernels for 0%

commit v1 on v0

v1 whole, which is shorter than its diff:
```python
import jax
import jax.numpy as jnp
from jax import lax
from jax.experimental import pallas as pl
from jax.experimental.pallas import tpu as pltpu
from jax.sharding import PartitionSpec as P

MESH = pl.DeviceIdType.MESH
F32 = jnp.float32
BF16 = jnp.bfloat16


def split(value):
    high = value.astype(BF16)
    return high, (value - high.astype(F32)).astype(BF16)


def dot(left, right):
    return jnp.dot(left, right, preferred_element_type=F32)


def masked_hopping(hop_ref, mask_ref, size):
    tiles = mask_ref.shape[-1]
    tile = size // tiles
    column = lax.broadcasted_iota(jnp.int32, (tile, size), 1)
    rows = []
    for i in range(tiles):
        keep = jnp.full((tile, size), mask_ref[0, i, tiles - 1].astype(F32))
        for j in range(tiles - 2, -1, -1):
            keep = jnp.where(column < (j + 1) * tile, mask_ref[0, i, j].astype(F32), keep)
        rows.append(hop_ref[i * tile : (i + 1) * tile, :] * keep)
    return jnp.concatenate(rows, axis=0)


def prepare(right_ref, left_ref, slot, real, imag):
    size = real.shape[0]
    half = size // 2
    for source, places in ((real, 0), (imag, 1)):
        high, low = split(source.T)
        for part, starts in ((high, (0, 4 * size)), (low, (2 * size,))):
            for start in starts:
                if places == 0:
                    right_ref[slot, start : start + size, 0:size] = part
                    right_ref[slot, start + size : start + 2 * size, size : 2 * size] = part
                else:
                    right_ref[slot, start : start + size, size : 2 * size] = -part
                    right_ref[slot, start + size : start + 2 * size, 0:size] = part
        high, low = split(source)
        for part, starts in ((high, (0, 2 * half)), (low, (4 * half,))):
            for g in range(2):
                for h in range(2):
                    block = part[g * half : (g + 1) * half, h * half : (h + 1) * half]
                    for start in starts:
                        if places == 0:
                            left_ref[slot, g, h, 0:half, start : start + half] = block
                            left_ref[slot, g, h, half : 2 * half, start + half : start + 2 * half] = block
                        else:
                            left_ref[slot, g, h, 0:half, start + half : start + 2 * half] = -block
                            left_ref[slot, g, h, half : 2 * half, start : start + half] = block


def half_times_adjoint(right_ref, slot, middle):
    size = middle.shape[-1]
    real_high, real_low = split(middle[0])
    imag_high, imag_low = split(middle[1])
    left = jnp.concatenate([real_high, imag_high, real_high, imag_high, real_low, imag_low], axis=1)
    product = dot(left, right_ref[slot])
    stacked = jnp.concatenate([product[:, 0:size], product[:, size : 2 * size]], axis=0)
    high, low = split(stacked)
    return jnp.concatenate([high, low, high], axis=0)


def kernel(
    retarded_hbm, lesser_hbm, hop_hbm, mask_ref, offsets_ref, coupling_ref, occupation_ref,
    out_hbm,
    held, partial_out, partial_in, retarded, hop, incoming, result, right_ref, left_ref,
    load_sem, near_send, near_recv, part_send, part_recv, chain_send, chain_recv, out_sem, gate,
):
    slab = lax.axis_index("slab")
    slabs = lax.axis_size("slab")
    place = lax.axis_index("energy")
    places = lax.axis_size("energy")
    core = lax.rem(place, 2)
    sign = 2 * core - 1
    size = retarded.shape[-1]
    half = size // 2

    def ring(index):
        return lax.rem(index + places, places)

    partner = place - sign
    across = ring(place + sign)
    ahead = ring(place + 2 * sign)
    behind = ring(place - 2 * sign)
    up = lax.rem(slab + 1, slabs)
    down = lax.rem(slab + slabs - 1, slabs)

    loads = [
        pltpu.make_async_copy(lesser_hbm.at[0], held.at[0], load_sem.at[0]),
        pltpu.make_async_copy(retarded_hbm.at[0], retarded, load_sem.at[1]),
        pltpu.make_async_copy(hop_hbm.at[0], hop, load_sem.at[2]),
    ]
    for load in loads:
        load.start()

    barrier = pltpu.get_barrier_semaphore()
    for other in (partner, across, ahead, behind):
        pl.semaphore_signal(barrier, inc=1, device_id={"slab": slab, "energy": other}, device_id_type=MESH)
    for other in (up, down):
        pl.semaphore_signal(barrier, inc=1, device_id={"slab": other, "energy": place}, device_id_type=MESH)
    pl.semaphore_wait(barrier, 6)

    def near_copy(slot, other):
        return pltpu.make_async_remote_copy(
            src_ref=lesser_hbm.at[0], dst_ref=held.at[slot],
            send_sem=near_send.at[slot - 1], recv_sem=near_recv.at[slot - 1],
            device_id={"slab": slab, "energy": other}, device_id_type=MESH,
        )

    to_partner = near_copy(1, partner)
    to_across = near_copy(2, across)
    to_partner.start()
    to_across.start()

    def part_copy(role, u):
        other = ahead if role == 0 else behind
        return pltpu.make_async_remote_copy(
            src_ref=partial_out.at[role, u], dst_ref=partial_in.at[role, u],
            send_sem=part_send.at[role, u], recv_sem=part_recv.at[role, u],
            device_id={"slab": slab, "energy": other}, device_id_type=MESH,
        )

    def chain_copy(u, g):
        rows = pl.ds(g * half, half)
        return pltpu.make_async_remote_copy(
            src_ref=result.at[u, :, rows, :], dst_ref=incoming.at[u, :, rows, :],
            send_sem=chain_send.at[u, g], recv_sem=chain_recv.at[u, g],
            device_id={"slab": up, "energy": place}, device_id_type=MESH,
        )

    modes = offsets_ref.shape[0]
    steps = [offsets_ref[k] for k in range(modes)]
    absorb = [coupling_ref[k] * occupation_ref[k] for k in range(modes)]
    emit = [coupling_ref[k] * (occupation_ref[k] + 1.0) for k in range(modes)]

    def weight(distance, above):
        total = jnp.float32(0.0)
        for k in range(modes):
            factor = jnp.where(above == 1, emit[k], absorb[k])
            total = total + jnp.where(steps[k] == distance, factor, 0.0)
        return total

    def inside(index):
        return jnp.where((index >= 0) & (index < places), 1.0, 0.0).astype(F32)

    loads[1].wait()
    loads[2].wait()
    mask_high, mask_low = split(masked_hopping(hop, mask_ref, size))
    hopping = jnp.concatenate([mask_high, mask_low, mask_high], axis=0)

    def operands(u, carry):
        real, imag = retarded[u, 0], retarded[u, 1]
        prepare(right_ref, left_ref, u, real, imag)
        high, low = split(jnp.concatenate([real, imag], axis=0))
        coupled = dot(jnp.concatenate([high, high, low], axis=1), hopping)
        prepare(right_ref, left_ref, 2 + u, coupled[0:size], coupled[size : 2 * size])
        return carry

    loads[0].wait()
    to_partner.wait()
    above_ahead = 1 - core
    above_behind = core
    for u in range(2):
        total = None
        for slot, reach in ((0, 4), (1, 6)):
            for b in range(2):
                term = weight(reach + sign * (u - b), above_ahead) * held[slot, b]
                total = term if total is None else total + term
        partial_out[0, u] = total

    @pl.when(core == 0)
    def _():
        for u in range(2):
            part_copy(0, u).start()

    lax.fori_loop(0, 2, operands, 0)

    to_across.wait()
    across_valid = inside(place + sign)
    for u in range(2):
        total = None
        for slot, reach in ((0, 4), (1, 2), (2, 6)):
            for b in range(2):
                factor = weight(reach - sign * (u - b), above_behind)
                if slot == 2:
                    factor = factor * across_valid
                term = factor * held[slot, b]
                total = term if total is None else total + term
        partial_out[1, u] = total

        @pl.when(core == 0)
        def _():
            part_copy(1, u).start()

    @pl.when(core == 1)
    def _():
        pl.semaphore_wait(gate, 1)
        for u in range(2):
            for role in range(2):
                part_copy(role, u).start()

    ahead_valid = inside(place - 2 * sign)
    behind_valid = inside(place + 2 * sign)

    def congruence(slot, middle_of, base_of, store):
        rights = [half_times_adjoint(right_ref, slot, middle_of(h)) for h in range(2)]
        for g in range(2):
            total = base_of(g)
            for h in range(2):
                product = dot(left_ref[slot, g, h], rights[h])
                total = product if total is None else total + product
            store(g, total)

    def store_result(u):
        def store(g, total):
            rows = pl.ds(g * half, half)
            result[u, 0, rows, :] = total[0:half]
            result[u, 1, rows, :] = total[half : 2 * half]

        return store

    for u in range(2):
        local = weight(1, 1 - u) * held[0, 1 - u]
        for b in range(2):
            local = local + weight(2 - sign * (b - u), 1 - core) * held[1, b]
        for role in range(2):
            part_copy(role, u).wait_recv()
        local = local + ahead_valid * partial_in[0, u] + behind_valid * partial_in[1, u]
        held[2, u] = local
        congruence(
            u,
            lambda h, u=u: held[2, u, :, h * half : (h + 1) * half, :],
            lambda g: None,
            store_result(u),
        )

        @pl.when(slab == 0)
        def _():
            for g in range(2):
                chain_copy(u, g).start()

        if u == 0:
            for role in range(2):
                for v in range(2):
                    part_copy(role, v).wait_send()

            @pl.when(core == 0)
            def _():
                pl.semaphore_signal(gate, inc=1, device_id={"slab": slab, "energy": partner}, device_id_type=MESH)

    @pl.when(slab > 0)
    def _():
        def advance(u, carry):
            rights = []
            for h in range(2):
                chain_copy(u, h).wait_recv()
                rights.append(half_times_adjoint(right_ref, 2 + u, incoming[u, :, h * half : (h + 1) * half, :]))
            for g in range(2):
                rows = pl.ds(g * half, half)
                total = jnp.concatenate([result[u, 0, rows, :], result[u, 1, rows, :]], axis=0)
                for h in range(2):
                    total = total + dot(left_ref[2 + u, g, h], rights[h])
                store_result(u)(g, total)

                @pl.when(slab < slabs - 1)
                def _():
                    chain_copy(u, g).start()

            return carry

        lax.fori_loop(0, 2, advance, 0)

    writes = [pltpu.make_async_copy(result.at[u], out_hbm.at[0, u], out_sem.at[u]) for u in range(2)]
    for write in writes:
        write.start()

    @pl.when(slab < slabs - 1)
    def _():
        for u in range(2):
            for g in range(2):
                chain_copy(u, g).wait_send()

    for write in writes:
        write.wait()


def body(retarded, lesser_prev, hopping, hop_mask, offsets, coupling, occupation):
    size = retarded.shape[-1]
    half = size // 2
    any_space = pl.BlockSpec(memory_space=pl.ANY)
    scalars = pl.BlockSpec(memory_space=pltpu.SMEM)
    dma = pltpu.SemaphoreType.DMA
    return pl.pallas_call(
        kernel,
        out_shape=jax.ShapeDtypeStruct(retarded.shape, F32),
        in_specs=[any_space] * 3 + [scalars] * 4,
        out_specs=any_space,
        scratch_shapes=[
            pltpu.VMEM((3, 2, 2, size, size), F32),
            pltpu.VMEM((2, 2, 2, size, size), F32),
            pltpu.VMEM((2, 2, 2, size, size), F32),
            pltpu.VMEM((2, 2, size, size), F32),
            pltpu.VMEM((size, size), F32),
            pltpu.VMEM((2, 2, size, size), F32),
            pltpu.VMEM((2, 2, size, size), F32),
            pltpu.VMEM((4, 6 * size, 2 * size), BF16),
            pltpu.VMEM((4, 2, 2, size, 6 * half), BF16),
            dma((3,)),
            dma((2,)),
            dma((2,)),
            dma((2, 2)),
            dma((2, 2)),
            dma((2, 2)),
            dma((2, 2)),
            dma((2,)),
            pltpu.SemaphoreType.REGULAR,
        ],
        compiler_params=pltpu.CompilerParams(
            collective_id=0, has_side_effects=True, vmem_limit_bytes=60 * 1024 * 1024
        ),
    )(retarded, lesser_prev, hopping, hop_mask, offsets, coupling, occupation)


def solution(mesh):
    return jax.shard_map(
        body,
        mesh=mesh,
        in_specs=(
            P("slab", "energy", None, None, None),
            P("slab", "energy", None, None, None),
            P("slab", None, None),
            P("slab", None, None),
            P(),
            P(),
            P(),
        ),
        out_specs=P("slab", "energy", None, None, None),
        check_vma=False,
    )
```

time: 346 us -> 127 us (0.37)
  the two profiles are of different devices: /device:TPU:486 before, /device:TPU:449 now
where the time goes in v1:
time: 127 us
  Pallas kernels  125 us (98%)
  local copies, waits for them, and re-layouts  2.29 us (2%)
    pallas_call x1, Pallas kernels, body(): pl.pallas_call(kernel, out_shape=jax.ShapeDtypeStruct(retarded.shape, F32...  125 us

profile of v1, /device:TPU:449, one launch (start us, length us, event | category | flops | bytes accessed | tf_op | source)
XLA Modules:
  0.0 126.9 jit_solution(12463981321702007476)
XLA Ops:
  0.0 124.6 %shard_map.73 = f32[1,2,2,256,256]{4,3,2,1,0:T(8,128)} custom-call(f32[1,2,2,256,256]{4,3,2,1,0:T(8,128)} %retarded_hbm.1, f32[1,2,2,256,256]{4,3,2,1,0:T(8,128)} %lesser_hbm.1, f32[1,256,256]{2,1,0:T(8,128)} %hop_hbm.1, s32[1,4,4]{2,1,0:T(4,128)} %mask_ref.1, s32[3]{0:T(128)} %offsets_ref.1, f32[3]{0:T(128)} %coupling_ref.1, f32[3]{0:T(128)} %occupation_ref.1), custom_call_target="tpu_custom_call" | custom-call | tf_op jit(solution)/shard_map/pallas_call | solution.py:303
  124.6 2.3 %copy.9 = f32[1,2,2,256,256]{4,3,2,1,0:T(8,128)} copy(f32[1,2,2,256,256]{4,3,2,1,0:T(8,128)} %shard_map.73) | data formatting | bytes 2097152

commit v2 on v1

--- a/solution.py
+++ b/solution.py
@@ -8,6 +8,8 @@
 MESH = pl.DeviceIdType.MESH
 F32 = jnp.float32
 BF16 = jnp.bfloat16
+HEAD = 3
+CHUNKS = 8
 
 
 def split(value):
@@ -72,10 +74,13 @@
 
 def kernel(
     retarded_hbm, lesser_hbm, hop_hbm, mask_ref, offsets_ref, coupling_ref, occupation_ref,
-    out_hbm,
-    held, partial_out, partial_in, retarded, hop, incoming, result, right_ref, left_ref,
-    load_sem, near_send, near_recv, part_send, part_recv, chain_send, chain_recv, out_sem, gate,
+    out_ref,
+    held, partial_out, partial_in, retarded, hop, incoming, carried, chained, chained_in,
+    right_ref, left_ref,
+    load_sem, near_send, near_recv, part_send, part_recv, chain_send, chain_recv, cast_send, cast_recv,
+    prod_send, prod_recv, gate, turn,
 ):
+    result = out_ref.at[0]
     slab = lax.axis_index("slab")
     slabs = lax.axis_size("slab")
     place = lax.axis_index("energy")
@@ -84,6 +89,8 @@
     sign = 2 * core - 1
     size = retarded.shape[-1]
     half = size // 2
+    chunk = size // CHUNKS
+    last = slabs - 1
 
     def ring(index):
         return lax.rem(index + places, places)
@@ -92,8 +99,9 @@
     across = ring(place + sign)
     ahead = ring(place + 2 * sign)
     behind = ring(place - 2 * sign)
-    up = lax.rem(slab + 1, slabs)
-    down = lax.rem(slab + slabs - 1, slabs)
+
+    def plane(step):
+        return lax.rem(slab + step, slabs)
 
     loads = [
         pltpu.make_async_copy(lesser_hbm.at[0], held.at[0], load_sem.at[0]),
@@ -103,12 +111,20 @@
     for load in loads:
         load.start()
 
+    @pl.when(place - 2 * sign != ring(place - 2 * sign))
+    def _():
+        partial_in[0] = jnp.zeros_like(partial_in[0])
+
+    @pl.when(place + 2 * sign != ring(place + 2 * sign))
+    def _():
+        partial_in[1] = jnp.zeros_like(partial_in[1])
+
     barrier = pltpu.get_barrier_semaphore()
     for other in (partner, across, ahead, behind):
         pl.semaphore_signal(barrier, inc=1, device_id={"slab": slab, "energy": other}, device_id_type=MESH)
-    for other in (up, down):
-        pl.semaphore_signal(barrier, inc=1, device_id={"slab": other, "energy": place}, device_id_type=MESH)
-    pl.semaphore_wait(barrier, 6)
+    for step in (1, slabs - 1, last - HEAD + 1, slabs - last + HEAD - 1):
+        pl.semaphore_signal(barrier, inc=1, device_id={"slab": plane(step), "energy": place}, device_id_type=MESH)
+    pl.semaphore_wait(barrier, 8)
 
     def near_copy(slot, other):
         return pltpu.make_async_remote_copy(
@@ -119,24 +135,67 @@
 
     to_partner = near_copy(1, partner)
     to_across = near_copy(2, across)
+    has_across = (place + sign >= 0) & (place + sign < places)
+    has_ahead = (place + 2 * sign >= 0) & (place + 2 * sign < places)
+    has_behind = (place - 2 * sign >= 0) & (place - 2 * sign < places)
     to_partner.start()
-    to_across.start()
-
-    def part_copy(role, u):
+
+    @pl.when(has_across)
+    def _():
+        to_across.start()
+
+    @pl.when(jnp.logical_not(has_across))
+    def _():
+        held[2] = jnp.zeros_like(held[2])
+
+
+    def part_copy(role, u, p):
         other = ahead if role == 0 else behind
         return pltpu.make_async_remote_copy(
-            src_ref=partial_out.at[role, u], dst_ref=partial_in.at[role, u],
-            send_sem=part_send.at[role, u], recv_sem=part_recv.at[role, u],
+            src_ref=partial_out.at[role, u, p], dst_ref=partial_in.at[role, u, p],
+            send_sem=part_send.at[role, u, p], recv_sem=part_recv.at[role, u, p],
             device_id={"slab": slab, "energy": other}, device_id_type=MESH,
+        )
+
+    def slab_copy(source, target, send_sem, recv_sem, to):
+        return pltpu.make_async_remote_copy(
+            src_ref=source, dst_ref=target, send_sem=send_sem, recv_sem=recv_sem,
+            device_id={"slab": to, "energy": place}, device_id_type=MESH,
         )
 
     def chain_copy(u, g):
         rows = pl.ds(g * half, half)
-        return pltpu.make_async_remote_copy(
-            src_ref=result.at[u, :, rows, :], dst_ref=incoming.at[u, :, rows, :],
-            send_sem=chain_send.at[u, g], recv_sem=chain_recv.at[u, g],
-            device_id={"slab": up, "energy": place}, device_id_type=MESH,
-        )
+        return slab_copy(
+            result.at[u, :, rows, :], incoming.at[u, :, rows, :], chain_send.at[u, g], chain_recv.at[u, g], plane(1)
+        )
+
+    def prod_copy(u, g):
+        rows = pl.ds(g * half, half)
+        return slab_copy(
+            chained.at[u, :, rows, :], chained_in.at[u, :, rows, :], prod_send.at[u, g], prod_recv.at[u, g], plane(1)
+        )
+
+    def cast_copy(way, u, c):
+        rows = pl.ds(c * chunk, chunk)
+        to = HEAD if way == 0 else last
+        return slab_copy(
+            result.at[u, :, rows, :], carried.at[u, :, rows, :], cast_send.at[way, u, c], cast_recv.at[u, c], to
+        )
+
+    def relay_copy(u, c):
+        rows = pl.ds(c * chunk, chunk)
+        to = jnp.where(slab == HEAD, plane(1), plane(slabs - 1))
+        return slab_copy(
+            carried.at[u, :, rows, :], carried.at[u, :, rows, :], cast_send.at[0, u, c], cast_recv.at[u, c], to
+        )
+
+    first_head = slab == 0
+    second_head = slab == HEAD
+    is_head = first_head | second_head
+    is_caster = slab == HEAD - 1
+    chains_on = (slab != HEAD - 1) & (slab != last)
+    in_second = slab >= HEAD
+    relays = second_head | (slab >= last - 1)
 
     modes = offsets_ref.shape[0]
     steps = [offsets_ref[k] for k in range(modes)]
@@ -150,21 +209,29 @@
             total = total + jnp.where(steps[k] == distance, factor, 0.0)
         return total
 
-    def inside(index):
-        return jnp.where((index >= 0) & (index < places), 1.0, 0.0).astype(F32)
+    def hand_over(which):
+        pl.semaphore_signal(which, inc=1, device_id={"slab": slab, "energy": partner}, device_id_type=MESH)
 
     loads[1].wait()
     loads[2].wait()
     mask_high, mask_low = split(masked_hopping(hop, mask_ref, size))
     hopping = jnp.concatenate([mask_high, mask_low, mask_high], axis=0)
 
-    def operands(u, carry):
+    def couple(u, carry):
         real, imag = retarded[u, 0], retarded[u, 1]
-        prepare(right_ref, left_ref, u, real, imag)
         high, low = split(jnp.concatenate([real, imag], axis=0))
         coupled = dot(jnp.concatenate([high, high, low], axis=1), hopping)
-        prepare(right_ref, left_ref, 2 + u, coupled[0:size], coupled[size : 2 * size])
+        chained[u, 0] = coupled[0:size]
+        chained[u, 1] = coupled[size : 2 * size]
+
+        @pl.when(second_head & (core == 0))
+        def _():
+            for g in range(2):
+                prod_copy(u, g).start()
+
         return carry
+
+    lax.fori_loop(0, 2, couple, 0)
 
     loads[0].wait()
     to_partner.wait()
@@ -178,39 +245,126 @@
                 total = term if total is None else total + term
         partial_out[0, u] = total
 
-    @pl.when(core == 0)
+    @pl.when((core == 0) & has_ahead)
     def _():
         for u in range(2):
-            part_copy(0, u).start()
+            for p in range(2):
+                part_copy(0, u, p).start()
+
+    @pl.when((core == 1) & has_ahead)
+    def _():
+        part_copy(0, 0, 0).start()
+
+    def operands(u, carry):
+        prepare(right_ref, left_ref, u, retarded[u, 0], retarded[u, 1])
+        prepare(right_ref, left_ref, 2 + u, chained[u, 0], chained[u, 1])
+        return carry
 
     lax.fori_loop(0, 2, operands, 0)
 
-    to_across.wait()
-    across_valid = inside(place + sign)
+    def products_sent():
+        for u in range(2):
+            for g in range(2):
+                prod_copy(u, g).wait_send()
+
+    def multiply(u):
+        rights = []
+        for h in range(2):
+            prod_copy(u, h).wait_recv()
+            rows = pl.ds(h * half, half)
+            high, low = split(jnp.concatenate([chained_in[u, 0, rows, :], chained_in[u, 1, rows, :]], axis=0))
+            rights.append(jnp.concatenate([high, low, high], axis=0))
+        for g in range(2):
+            total = dot(left_ref[2 + u, g, 0], rights[0]) + dot(left_ref[2 + u, g, 1], rights[1])
+            rows = pl.ds(g * half, half)
+            chained[u, 0, rows, :] = total[0:half]
+            chained[u, 1, rows, :] = total[half : 2 * half]
+
+        @pl.when(slab < last)
+        def _():
+            @pl.when((core == 1) & (u == 0))
+            def _():
+                pl.semaphore_wait(turn.at[0], 1)
+
+            for g in range(2):
+                prod_copy(u, g).start()
+
+    early = (slab == HEAD + 1) & (core == 0)
+
+    @pl.when(second_head & (core == 0))
+    def _():
+        products_sent()
+        hand_over(turn.at[0])
+
+    @pl.when(second_head & (core == 1))
+    def _():
+        pl.semaphore_wait(turn.at[0], 1)
+        for u in range(2):
+            for g in range(2):
+                prod_copy(u, g).start()
+
+    @pl.when(early)
+    def _():
+        multiply(0)
+
+    @pl.when(has_across)
+    def _():
+        to_across.wait()
+
     for u in range(2):
         total = None
         for slot, reach in ((0, 4), (1, 2), (2, 6)):
             for b in range(2):
                 factor = weight(reach - sign * (u - b), above_behind)
-                if slot == 2:
-                    factor = factor * across_valid
                 term = factor * held[slot, b]
                 total = term if total is None else total + term
         partial_out[1, u] = total
 
-        @pl.when(core == 0)
-        def _():
-            part_copy(1, u).start()
+        @pl.when((core == 0) & has_behind)
+        def _():
+            for p in range(2):
+                part_copy(1, u, p).start()
+
+    @pl.when(in_second)
+    def _():
+        def product(u, carry):
+            @pl.when((slab > HEAD) & jnp.logical_not(early & (u == 0)))
+            def _():
+                multiply(u)
+
+            prepare(right_ref, left_ref, 4 + u, chained[u, 0], chained[u, 1])
+            return carry
+
+        lax.fori_loop(0, 2, product, 0)
+
+        @pl.when((core == 0) & (slab > HEAD) & (slab < last))
+        def _():
+            products_sent()
+            hand_over(turn.at[0])
 
     @pl.when(core == 1)
     def _():
-        pl.semaphore_wait(gate, 1)
-        for u in range(2):
-            for role in range(2):
-                part_copy(role, u).start()
-
-    ahead_valid = inside(place - 2 * sign)
-    behind_valid = inside(place + 2 * sign)
+        pl.semaphore_wait(gate.at[0], 1)
+
+        @pl.when(has_behind)
+        def _():
+            for u in range(2):
+                for p in range(2):
+                    part_copy(1, u, p).start()
+
+        pl.semaphore_wait(gate.at[1], 1)
+
+        @pl.when(has_ahead)
+        def _():
+            for u in range(2):
+                for p in range(2):
+                    if u + p > 0:
+                        part_copy(0, u, p).start()
+
+    @pl.when((core == 1) & in_second & (slab < last))
+    def _():
+        products_sent()
+        hand_over(turn.at[2])
 
     def congruence(slot, middle_of, base_of, store):
         rights = [half_times_adjoint(right_ref, slot, middle_of(h)) for h in range(2)]
@@ -221,77 +375,180 @@
                 total = product if total is None else total + product
             store(g, total)
 
-    def store_result(u):
-        def store(g, total):
-            rows = pl.ds(g * half, half)
-            result[u, 0, rows, :] = total[0:half]
-            result[u, 1, rows, :] = total[half : 2 * half]
-
-        return store
+    def stacked_result(u, g):
+        rows = pl.ds(g * half, half)
+        return jnp.concatenate([result[u, 0, rows, :], result[u, 1, rows, :]], axis=0)
+
+    def store_result(u, g, total):
+        rows = pl.ds(g * half, half)
+        result[u, 0, rows, :] = total[0:half]
+        result[u, 1, rows, :] = total[half : 2 * half]
+
+    def send_on(u, g):
+        @pl.when(chains_on)
+        def _():
+            chain_copy(u, g).start()
+
+        @pl.when(is_caster)
+        def _():
+            for c in range(CHUNKS // 2):
+                for way in range(2):
+                    cast_copy(way, u, g * (CHUNKS // 2) + c).start()
+
+    def wait_sent():
+        @pl.when(chains_on)
+        def _():
+            for u in range(2):
+                for g in range(2):
+                    chain_copy(u, g).wait_send()
+
+        @pl.when(is_caster)
+        def _():
+            for u in range(2):
+                for c in range(CHUNKS):
+                    for way in range(2):
+                        cast_copy(way, u, c).wait_send()
+
+    def parts_sent(role, goes):
+        @pl.when(goes)
+        def _():
+            for v in range(2):
+                for p in range(2):
+                    part_copy(role, v, p).wait_send()
+
+    def my_turn():
+        @pl.when((core == 1) & (slab < last))
+        def _():
+            pl.semaphore_wait(turn.at[1], 1)
+
+        @pl.when((core == 0) & in_second & (slab < last))
+        def _():
+            pl.semaphore_wait(turn.at[2], 1)
+
+    def pass_turn():
+        @pl.when((core == 0) & (slab < last))
+        def _():
+            wait_sent()
+            hand_over(turn.at[1])
 
     for u in range(2):
+        if u == 0:
+
+            @pl.when(core == 0)
+            def _():
+                parts_sent(0, has_ahead)
+                hand_over(gate.at[0])
+
         local = weight(1, 1 - u) * held[0, 1 - u]
         for b in range(2):
             local = local + weight(2 - sign * (b - u), 1 - core) * held[1, b]
-        for role in range(2):
-            part_copy(role, u).wait_recv()
-        local = local + ahead_valid * partial_in[0, u] + behind_valid * partial_in[1, u]
+        for role, comes in ((0, has_behind), (1, has_ahead)):
+
+            @pl.when(comes)
+            def _():
+                for p in range(2):
+                    part_copy(role, u, p).wait_recv()
+
+        local = local + partial_in[0, u] + partial_in[1, u]
         held[2, u] = local
         congruence(
             u,
             lambda h, u=u: held[2, u, :, h * half : (h + 1) * half, :],
             lambda g: None,
-            store_result(u),
-        )
-
-        @pl.when(slab == 0)
-        def _():
-            for g in range(2):
-                chain_copy(u, g).start()
+            lambda g, total, u=u: store_result(u, g, total),
+        )
 
         if u == 0:
-            for role in range(2):
-                for v in range(2):
-                    part_copy(role, v).wait_send()
 
             @pl.when(core == 0)
             def _():
-                pl.semaphore_signal(gate, inc=1, device_id={"slab": slab, "energy": partner}, device_id_type=MESH)
-
-    @pl.when(slab > 0)
-    def _():
-        def advance(u, carry):
+                parts_sent(1, has_behind)
+                hand_over(gate.at[1])
+
+        @pl.when(is_head)
+        def _():
+            if u == 0:
+                my_turn()
+            for g in range(2):
+                send_on(u, g)
+
+        if u == 1:
+
+            @pl.when(is_head)
+            def _():
+                pass_turn()
+
+    def relay(u):
+        for c in range(CHUNKS):
+            relay_copy(u, c).wait_recv()
+            relay_copy(u, c).start()
+
+    @pl.when(slab == last)
+    def _():
+        for u in range(2):
+            relay(u)
+
+    def advance(u, carry):
+        @pl.when(jnp.logical_not(is_head))
+        def _():
             rights = []
             for h in range(2):
                 chain_copy(u, h).wait_recv()
                 rights.append(half_times_adjoint(right_ref, 2 + u, incoming[u, :, h * half : (h + 1) * half, :]))
             for g in range(2):
-                rows = pl.ds(g * half, half)
-                total = jnp.concatenate([result[u, 0, rows, :], result[u, 1, rows, :]], axis=0)
+                total = stacked_result(u, g)
                 for h in range(2):
                     total = total + dot(left_ref[2 + u, g, h], rights[h])
-                store_result(u)(g, total)
-
-                @pl.when(slab < slabs - 1)
-                def _():
-                    chain_copy(u, g).start()
-
+                store_result(u, g, total)
+                if g == 0:
+
+                    @pl.when(u == 0)
+                    def _():
+                        my_turn()
+
+                send_on(u, g)
+
+        @pl.when(second_head | (slab == last - 1))
+        def _():
+            relay(u)
+
+        @pl.when(jnp.logical_not(is_head) & (u == 1))
+        def _():
+            pass_turn()
+
+        return carry
+
+    lax.fori_loop(0, 2, advance, 0)
+
+    @pl.when(core == 1)
+    def _():
+        wait_sent()
+        parts_sent(0, has_ahead)
+        parts_sent(1, has_behind)
+
+    @pl.when(in_second)
+    def _():
+        def apply(u, carry):
+            @pl.when(jnp.logical_not(relays))
+            def _():
+                for c in range(CHUNKS):
+                    relay_copy(u, c).wait_recv()
+
+            congruence(
+                4 + u,
+                lambda h: carried[u, :, h * half : (h + 1) * half, :],
+                lambda g: stacked_result(u, g),
+                lambda g, total: store_result(u, g, total),
+            )
             return carry
 
-        lax.fori_loop(0, 2, advance, 0)
-
-    writes = [pltpu.make_async_copy(result.at[u], out_hbm.at[0, u], out_sem.at[u]) for u in range(2)]
-    for write in writes:
-        write.start()
-
-    @pl.when(slab < slabs - 1)
-    def _():
-        for u in range(2):
-            for g in range(2):
-                chain_copy(u, g).wait_send()
-
-    for write in writes:
-        write.wait()
+        lax.fori_loop(0, 2, apply, 0)
+
+        @pl.when(relays)
+        def _():
+            for u in range(2):
+                for c in range(CHUNKS):
+                    relay_copy(u, c).wait_send()
 
 
 def body(retarded, lesser_prev, hopping, hop_mask, offsets, coupling, occupation):
@@ -302,9 +559,9 @@
     dma = pltpu.SemaphoreType.DMA
     return pl.pallas_call(
         kernel,
-        out_shape=jax.ShapeDtypeStruct(retarded.shape, F32),
+        out_shape=pltpu.VMEM(retarded.shape, F32),
         in_specs=[any_space] * 3 + [scalars] * 4,
-        out_specs=any_space,
+        out_specs=pl.BlockSpec(memory_space=pltpu.VMEM),
         scratch_shapes=[
             pltpu.VMEM((3, 2, 2, size, size), F32),
             pltpu.VMEM((2, 2, 2, size, size), F32),
@@ -313,17 +570,23 @@
             pltpu.VMEM((size, size), F32),
             pltpu.VMEM((2, 2, size, size), F32),
             pltpu.VMEM((2, 2, size, size), F32),
-            pltpu.VMEM((4, 6 * size, 2 * size), BF16),
-            pltpu.VMEM((4, 2, 2, size, 6 * half), BF16),
+            pltpu.VMEM((2, 2, size, size), F32),
+            pltpu.VMEM((2, 2, size, size), F32),
+            pltpu.VMEM((6, 6 * size, 2 * size), BF16),
+            pltpu.VMEM((6, 2, 2, size, 6 * half), BF16),
             dma((3,)),
             dma((2,)),
             dma((2,)),
+            dma((2, 2, 2)),
+            dma((2, 2, 2)),
             dma((2, 2)),
             dma((2, 2)),
+            dma((2, 2, CHUNKS)),
+            dma((2, CHUNKS)),
             dma((2, 2)),
             dma((2, 2)),
-            dma((2,)),
-            pltpu.SemaphoreType.REGULAR,
+            pltpu.SemaphoreType.REGULAR((2,)),
+            pltpu.SemaphoreType.REGULAR((3,)),
         ],
         compiler_params=pltpu.CompilerParams(
             collective_id=0, has_side_effects=True, vmem_limit_bytes=60 * 1024 * 1024

time: 127 us -> 97.3 us (0.77)
  Pallas kernels: 125 us -> 96.1 us
  local copies, waits for them, and re-layouts: 2.29 us -> 0.97 us
    pallas_call x1, Pallas kernels: 125 us -> 96.1 us  [body(): pl.pallas_call(kernel, out_shape=pltpu.VMEM(retarded.shape, F32), in_spec...]
    unnamed x1, local copies, waits for them, and re-layouts: 2.29 us -> 0.97 us
where the time goes in v2:
time: 97.3 us; the launch traced here: 97.1 us
  Pallas kernels  96.1 us (99%)
    pallas_call x1, Pallas kernels, body(): pl.pallas_call(kernel, out_shape=pltpu.VMEM(retarded.shape, F32), in_spec...  96.1 us

profile of v2, /device:TPU:449, one launch (start us, length us, event | category | flops | bytes accessed | tf_op | source)
XLA Modules:
  0.0 97.1 jit_solution(13797393176339118752)
XLA Ops:
  0.0 96.1 %shard_map.73 = f32[1,2,2,256,256]{4,3,2,1,0:T(8,128)S(1)} custom-call(f32[1,2,2,256,256]{4,3,2,1,0:T(8,128)} %retarded_hbm.1, f32[1,2,2,256,256]{4,3,2,1,0:T(8,128)} %lesser_hbm.1, f32[1,256,256]{2,1,0:T(8,128)} %hop_hbm.1, s32[1,4,4]{2,1,0:T(4,128)} %mask_ref.1, s32[3]{0:T(128)} %offsets_ref.1, f32[3]{0:T(128)} %coupling_ref.1, f32[3]{0:T(128)} %occupation_ref.1), custom_call_target="tpu_custom_call" | custom-call | tf_op jit(solution)/shard_map/pallas_call | solution.py:560
  96.2 1.0 %copy.9 = f32[1,2,2,256,256]{4,3,2,1,0:T(8,128)} copy(f32[1,2,2,256,256]{4,3,2,1,0:T(8,128)S(1)} %shard_map.73) | data formatting | bytes 2097152

commit v3 on v2

--- a/solution.py
+++ b/solution.py
@@ -124,6 +124,22 @@
         pl.semaphore_signal(barrier, inc=1, device_id={"slab": slab, "energy": other}, device_id_type=MESH)
     for step in (1, slabs - 1, last - HEAD + 1, slabs - last + HEAD - 1):
         pl.semaphore_signal(barrier, inc=1, device_id={"slab": plane(step), "energy": place}, device_id_type=MESH)
+    loads[1].wait()
+    loads[2].wait()
+    mask_high, mask_low = split(masked_hopping(hop, mask_ref, size))
+    hopping = jnp.concatenate([mask_high, mask_low, mask_high], axis=0)
+
+    def couple(u, carry):
+        real, imag = retarded[u, 0], retarded[u, 1]
+        high, low = split(jnp.concatenate([real, imag], axis=0))
+        coupled = dot(jnp.concatenate([high, high, low], axis=1), hopping)
+        chained[u, 0] = coupled[0:size]
+        chained[u, 1] = coupled[size : 2 * size]
+
+        return carry
+
+    lax.fori_loop(0, 2, couple, 0)
+
     pl.semaphore_wait(barrier, 8)
 
     def near_copy(slot, other):
@@ -212,26 +228,11 @@
     def hand_over(which):
         pl.semaphore_signal(which, inc=1, device_id={"slab": slab, "energy": partner}, device_id_type=MESH)
 
-    loads[1].wait()
-    loads[2].wait()
-    mask_high, mask_low = split(masked_hopping(hop, mask_ref, size))
-    hopping = jnp.concatenate([mask_high, mask_low, mask_high], axis=0)
-
-    def couple(u, carry):
-        real, imag = retarded[u, 0], retarded[u, 1]
-        high, low = split(jnp.concatenate([real, imag], axis=0))
-        coupled = dot(jnp.concatenate([high, high, low], axis=1), hopping)
-        chained[u, 0] = coupled[0:size]
-        chained[u, 1] = coupled[size : 2 * size]
-
-        @pl.when(second_head & (core == 0))
-        def _():
+    @pl.when(second_head & (core == 0))
+    def _():
+        for u in range(2):
             for g in range(2):
                 prod_copy(u, g).start()
-
-        return carry
-
-    lax.fori_loop(0, 2, couple, 0)
 
     loads[0].wait()
     to_partner.wait()
@@ -262,10 +263,11 @@
 
     lax.fori_loop(0, 2, operands, 0)
 
-    def products_sent():
+    def products_sent(which):
         for u in range(2):
             for g in range(2):
                 prod_copy(u, g).wait_send()
+        hand_over(which)
 
     def multiply(u):
         rights = []
@@ -293,8 +295,7 @@
 
     @pl.when(second_head & (core == 0))
     def _():
-        products_sent()
-        hand_over(turn.at[0])
+        products_sent(turn.at[0])
 
     @pl.when(second_head & (core == 1))
     def _():
@@ -339,8 +340,7 @@
 
         @pl.when((core == 0) & (slab > HEAD) & (slab < last))
         def _():
-            products_sent()
-            hand_over(turn.at[0])
+            products_sent(turn.at[0])
 
     @pl.when(core == 1)
     def _():
@@ -351,6 +351,10 @@
             for u in range(2):
                 for p in range(2):
                     part_copy(1, u, p).start()
+
+        @pl.when(in_second & (slab < last))
+        def _():
+            products_sent(turn.at[2])
 
         pl.semaphore_wait(gate.at[1], 1)
 
@@ -360,11 +364,6 @@
                 for p in range(2):
                     if u + p > 0:
                         part_copy(0, u, p).start()
-
-    @pl.when((core == 1) & in_second & (slab < last))
-    def _():
-        products_sent()
-        hand_over(turn.at[2])
 
     def congruence(slot, middle_of, base_of, store):
         rights = [half_times_adjoint(right_ref, slot, middle_of(h)) for h in range(2)]
@@ -431,13 +430,17 @@
             wait_sent()
             hand_over(turn.at[1])
 
+    def relay(u):
+        for c in range(CHUNKS):
+            relay_copy(u, c).wait_recv()
+            relay_copy(u, c).start()
+
+    late = (slab == last) & (core == 1)
     for u in range(2):
-        if u == 0:
-
-            @pl.when(core == 0)
-            def _():
-                parts_sent(0, has_ahead)
-                hand_over(gate.at[0])
+
+        @pl.when(late)
+        def _():
+            relay(u)
 
         local = weight(1, 1 - u) * held[0, 1 - u]
         for b in range(2):
@@ -458,35 +461,57 @@
             lambda g, total, u=u: store_result(u, g, total),
         )
 
-        if u == 0:
-
-            @pl.when(core == 0)
-            def _():
-                parts_sent(1, has_behind)
-                hand_over(gate.at[1])
-
-        @pl.when(is_head)
-        def _():
+        def start(u=u):
             if u == 0:
                 my_turn()
             for g in range(2):
                 send_on(u, g)
 
+        pl.when(first_head)(start)
+        if u == 0:
+
+            @pl.when(core == 0)
+            def _():
+                parts_sent(0, has_ahead)
+                hand_over(gate.at[0])
+                parts_sent(1, has_behind)
+                hand_over(gate.at[1])
+
+        pl.when(second_head)(start)
         if u == 1:
 
             @pl.when(is_head)
             def _():
                 pass_turn()
 
-    def relay(u):
-        for c in range(CHUNKS):
-            relay_copy(u, c).wait_recv()
-            relay_copy(u, c).start()
+            @pl.when(second_head & (core == 1))
+            def _():
+                wait_sent()
+                hand_over(turn.at[3])
+
+            @pl.when(second_head & (core == 0))
+            def _():
+                pl.semaphore_wait(turn.at[3], 1)
+
+    def apply(u):
+        congruence(
+            4 + u,
+            lambda h: carried[u, :, h * half : (h + 1) * half, :],
+            lambda g: stacked_result(u, g),
+            lambda g, total: store_result(u, g, total),
+        )
 
     @pl.when(slab == last)
     def _():
-        for u in range(2):
-            relay(u)
+        def pass_and_use(u, carry):
+            @pl.when(jnp.logical_not(late))
+            def _():
+                relay(u)
+
+            apply(u)
+            return carry
+
+        lax.fori_loop(0, 2, pass_and_use, 0)
 
     def advance(u, carry):
         @pl.when(jnp.logical_not(is_head))
@@ -520,35 +545,33 @@
 
     lax.fori_loop(0, 2, advance, 0)
 
+    @pl.when((core == 1) & jnp.logical_not(second_head))
+    def _():
+        wait_sent()
+
     @pl.when(core == 1)
     def _():
-        wait_sent()
         parts_sent(0, has_ahead)
         parts_sent(1, has_behind)
 
-    @pl.when(in_second)
-    def _():
-        def apply(u, carry):
+    @pl.when(in_second & (slab < last))
+    def _():
+        def use(u, carry):
             @pl.when(jnp.logical_not(relays))
             def _():
                 for c in range(CHUNKS):
                     relay_copy(u, c).wait_recv()
 
-            congruence(
-                4 + u,
-                lambda h: carried[u, :, h * half : (h + 1) * half, :],
-                lambda g: stacked_result(u, g),
-                lambda g, total: store_result(u, g, total),
-            )
+            apply(u)
             return carry
 
-        lax.fori_loop(0, 2, apply, 0)
-
-        @pl.when(relays)
-        def _():
-            for u in range(2):
-                for c in range(CHUNKS):
-                    relay_copy(u, c).wait_send()
+        lax.fori_loop(0, 2, use, 0)
+
+    @pl.when(relays)
+    def _():
+        for u in range(2):
+            for c in range(CHUNKS):
+                relay_copy(u, c).wait_send()
 
 
 def body(retarded, lesser_prev, hopping, hop_mask, offsets, coupling, occupation):
@@ -586,7 +609,7 @@
             dma((2, 2)),
             dma((2, 2)),
             pltpu.SemaphoreType.REGULAR((2,)),
-            pltpu.SemaphoreType.REGULAR((3,)),
+            pltpu.SemaphoreType.REGULAR((4,)),
         ],
         compiler_params=pltpu.CompilerParams(
             collective_id=0, has_side_effects=True, vmem_limit_bytes=60 * 1024 * 1024

time: 97.3 us -> 89.6 us (0.921)
  the two profiles are of different devices: /device:TPU:449 before, /device:TPU:323 now
where the time goes in v3:
time: 89.6 us; the launch traced here: 89.4 us
  Pallas kernels  88.4 us (99%)
  local copies, waits for them, and re-layouts  0.97 us (1%)
    pallas_call x1, Pallas kernels, body(): pl.pallas_call(kernel, out_shape=pltpu.VMEM(retarded.shape, F32), in_spec...  88.4 us

profile of v3, /device:TPU:323, one launch (start us, length us, event | category | flops | bytes accessed | tf_op | source)
XLA Modules:
  0.0 89.4 jit_solution(15060602611801481847)
XLA Ops:
  0.0 88.4 %shard_map.73 = f32[1,2,2,256,256]{4,3,2,1,0:T(8,128)S(1)} custom-call(f32[1,2,2,256,256]{4,3,2,1,0:T(8,128)} %retarded_hbm.1, f32[1,2,2,256,256]{4,3,2,1,0:T(8,128)} %lesser_hbm.1, f32[1,256,256]{2,1,0:T(8,128)} %hop_hbm.1, s32[1,4,4]{2,1,0:T(4,128)} %mask_ref.1, s32[3]{0:T(128)} %offsets_ref.1, f32[3]{0:T(128)} %coupling_ref.1, f32[3]{0:T(128)} %occupation_ref.1), custom_call_target="tpu_custom_call" | custom-call | tf_op jit(solution)/shard_map/pallas_call | solution.py:583
  88.4 1.0 %copy.9 = f32[1,2,2,256,256]{4,3,2,1,0:T(8,128)} copy(f32[1,2,2,256,256]{4,3,2,1,0:T(8,128)S(1)} %shard_map.73) | data formatting | bytes 2097152

commit v4 on v3

--- a/solution.py
+++ b/solution.py
@@ -179,16 +179,22 @@
             device_id={"slab": to, "energy": place}, device_id_type=MESH,
         )
 
-    def chain_copy(u, g):
-        rows = pl.ds(g * half, half)
+    def rows_of(k):
+        return pl.ds(0, half) if k == 0 else pl.ds(half + (k - 1) * (half // 2), half // 2)
+
+    def pieces_of(g):
+        return (0,) if g == 0 else (1, 2)
+
+    def chain_copy(u, k):
+        rows = rows_of(k)
         return slab_copy(
-            result.at[u, :, rows, :], incoming.at[u, :, rows, :], chain_send.at[u, g], chain_recv.at[u, g], plane(1)
-        )
-
-    def prod_copy(u, g):
-        rows = pl.ds(g * half, half)
+            result.at[u, :, rows, :], incoming.at[u, :, rows, :], chain_send.at[u, k], chain_recv.at[u, k], plane(1)
+        )
+
+    def prod_copy(u, k):
+        rows = rows_of(k)
         return slab_copy(
-            chained.at[u, :, rows, :], chained_in.at[u, :, rows, :], prod_send.at[u, g], prod_recv.at[u, g], plane(1)
+            chained.at[u, :, rows, :], chained_in.at[u, :, rows, :], prod_send.at[u, k], prod_recv.at[u, k], plane(1)
         )
 
     def cast_copy(way, u, c):
@@ -231,8 +237,8 @@
     @pl.when(second_head & (core == 0))
     def _():
         for u in range(2):
-            for g in range(2):
-                prod_copy(u, g).start()
+            for k in range(3):
+                prod_copy(u, k).start()
 
     loads[0].wait()
     to_partner.wait()
@@ -265,14 +271,16 @@
 
     def products_sent(which):
         for u in range(2):
-            for g in range(2):
-                prod_copy(u, g).wait_send()
+            for k in range(3 - u):
+                prod_copy(u, k).wait_send()
         hand_over(which)
+        prod_copy(1, 2).wait_send()
 
     def multiply(u):
         rights = []
         for h in range(2):
-            prod_copy(u, h).wait_recv()
+            for k in pieces_of(h):
+                prod_copy(u, k).wait_recv()
             rows = pl.ds(h * half, half)
             high, low = split(jnp.concatenate([chained_in[u, 0, rows, :], chained_in[u, 1, rows, :]], axis=0))
             rights.append(jnp.concatenate([high, low, high], axis=0))
@@ -288,8 +296,8 @@
             def _():
                 pl.semaphore_wait(turn.at[0], 1)
 
-            for g in range(2):
-                prod_copy(u, g).start()
+            for k in range(3):
+                prod_copy(u, k).start()
 
     early = (slab == HEAD + 1) & (core == 0)
 
@@ -301,8 +309,8 @@
     def _():
         pl.semaphore_wait(turn.at[0], 1)
         for u in range(2):
-            for g in range(2):
-                prod_copy(u, g).start()
+            for k in range(3):
+                prod_copy(u, k).start()
 
     @pl.when(early)
     def _():
@@ -352,7 +360,7 @@
                 for p in range(2):
                     part_copy(1, u, p).start()
 
-        @pl.when(in_second & (slab < last))
+        @pl.when(second_head)
         def _():
             products_sent(turn.at[2])
 
@@ -364,6 +372,10 @@
                 for p in range(2):
                     if u + p > 0:
                         part_copy(0, u, p).start()
+
+        @pl.when((slab > HEAD) & (slab < last))
+        def _():
+            products_sent(turn.at[2])
 
     def congruence(slot, middle_of, base_of, store):
         rights = [half_times_adjoint(right_ref, slot, middle_of(h)) for h in range(2)]
@@ -386,7 +398,8 @@
     def send_on(u, g):
         @pl.when(chains_on)
         def _():
-            chain_copy(u, g).start()
+            for k in pieces_of(g):
+                chain_copy(u, k).start()
 
         @pl.when(is_caster)
         def _():
@@ -394,19 +407,32 @@
                 for way in range(2):
                     cast_copy(way, u, g * (CHUNKS // 2) + c).start()
 
-    def wait_sent():
+    def wait_sent(which=None):
         @pl.when(chains_on)
         def _():
             for u in range(2):
-                for g in range(2):
-                    chain_copy(u, g).wait_send()
+                for k in range(3 - u):
+                    chain_copy(u, k).wait_send()
 
         @pl.when(is_caster)
         def _():
             for u in range(2):
-                for c in range(CHUNKS):
+                for c in range(CHUNKS - 2 * u):
                     for way in range(2):
                         cast_copy(way, u, c).wait_send()
+
+        if which is not None:
+            hand_over(which)
+
+        @pl.when(chains_on)
+        def _():
+            chain_copy(1, 2).wait_send()
+
+        @pl.when(is_caster)
+        def _():
+            for c in range(CHUNKS - 2, CHUNKS):
+                for way in range(2):
+                    cast_copy(way, 1, c).wait_send()
 
     def parts_sent(role, goes):
         @pl.when(goes)
@@ -427,11 +453,10 @@
     def pass_turn():
         @pl.when((core == 0) & (slab < last))
         def _():
-            wait_sent()
-            hand_over(turn.at[1])
-
-    def relay(u):
-        for c in range(CHUNKS):
+            wait_sent(turn.at[1])
+
+    def relay(u, first=0, end=CHUNKS):
+        for c in range(first, end):
             relay_copy(u, c).wait_recv()
             relay_copy(u, c).start()
 
@@ -474,10 +499,15 @@
             def _():
                 parts_sent(0, has_ahead)
                 hand_over(gate.at[0])
+
+        pl.when(second_head)(start)
+        if u == 0:
+
+            @pl.when(core == 0)
+            def _():
                 parts_sent(1, has_behind)
                 hand_over(gate.at[1])
 
-        pl.when(second_head)(start)
         if u == 1:
 
             @pl.when(is_head)
@@ -486,8 +516,7 @@
 
             @pl.when(second_head & (core == 1))
             def _():
-                wait_sent()
-                hand_over(turn.at[3])
+                wait_sent(turn.at[3])
 
             @pl.when(second_head & (core == 0))
             def _():
@@ -516,26 +545,34 @@
     def advance(u, carry):
         @pl.when(jnp.logical_not(is_head))
         def _():
-            rights = []
             for h in range(2):
-                chain_copy(u, h).wait_recv()
-                rights.append(half_times_adjoint(right_ref, 2 + u, incoming[u, :, h * half : (h + 1) * half, :]))
-            for g in range(2):
-                total = stacked_result(u, g)
-                for h in range(2):
-                    total = total + dot(left_ref[2 + u, g, h], rights[h])
-                store_result(u, g, total)
-                if g == 0:
-
-                    @pl.when(u == 0)
+                for k in pieces_of(h):
+                    chain_copy(u, k).wait_recv()
+                right = half_times_adjoint(right_ref, 2 + u, incoming[u, :, h * half : (h + 1) * half, :])
+                for g in range(2):
+                    store_result(u, g, stacked_result(u, g) + dot(left_ref[2 + u, g, h], right))
+                    if h == 1:
+                        if g == 0:
+
+                            @pl.when(u == 0)
+                            def _():
+                                my_turn()
+
+                        send_on(u, g)
+                if h == 0:
+
+                    @pl.when(slab == last - 1)
                     def _():
-                        my_turn()
-
-                send_on(u, g)
-
-        @pl.when(second_head | (slab == last - 1))
+                        relay(u, 0, CHUNKS // 2)
+
+
+        @pl.when(second_head)
         def _():
             relay(u)
+
+        @pl.when(slab == last - 1)
+        def _():
+            relay(u, CHUNKS // 2)
 
         @pl.when(jnp.logical_not(is_head) & (u == 1))
         def _():
@@ -602,12 +639,12 @@
             dma((2,)),
             dma((2, 2, 2)),
             dma((2, 2, 2)),
-            dma((2, 2)),
-            dma((2, 2)),
+            dma((2, 3)),
+            dma((2, 3)),
             dma((2, 2, CHUNKS)),
             dma((2, CHUNKS)),
-            dma((2, 2)),
-            dma((2, 2)),
+            dma((2, 3)),
+            dma((2, 3)),
             pltpu.SemaphoreType.REGULAR((2,)),
             pltpu.SemaphoreType.REGULAR((4,)),
         ],

time: 89.6 us -> 88.5 us (0.988)
  the two profiles are of different devices: /device:TPU:323 before, /device:TPU:389 now
where the time goes in v4:
time: 88.5 us; the launch traced here: 88.4 us
  Pallas kernels  87.4 us (99%)
  local copies, waits for them, and re-layouts  0.97 us (1%)
    pallas_call x1, Pallas kernels, body(): pl.pallas_call(kernel, out_shape=pltpu.VMEM(retarded.shape, F32), in_spec...  87.4 us

profile of v4, /device:TPU:389, one launch (start us, length us, event | category | flops | bytes accessed | tf_op | source)
XLA Modules:
  0.0 88.4 jit_solution(14803997577522995875)
XLA Ops:
  0.0 87.4 %shard_map.73 = f32[1,2,2,256,256]{4,3,2,1,0:T(8,128)S(1)} custom-call(f32[1,2,2,256,256]{4,3,2,1,0:T(8,128)} %retarded_hbm.1, f32[1,2,2,256,256]{4,3,2,1,0:T(8,128)} %lesser_hbm.1, f32[1,256,256]{2,1,0:T(8,128)} %hop_hbm.1, s32[1,4,4]{2,1,0:T(4,128)} %mask_ref.1, s32[3]{0:T(128)} %offsets_ref.1, f32[3]{0:T(128)} %coupling_ref.1, f32[3]{0:T(128)} %occupation_ref.1), custom_call_target="tpu_custom_call" | custom-call | tf_op jit(solution)/shard_map/pallas_call | solution.py:620
  87.4 1.0 %copy.9 = f32[1,2,2,256,256]{4,3,2,1,0:T(8,128)} copy(f32[1,2,2,256,256]{4,3,2,1,0:T(8,128)S(1)} %shard_map.73) | data formatting | bytes 2097152

commit v5 on v4

--- a/solution.py
+++ b/solution.py
@@ -180,7 +180,7 @@
         )
 
     def rows_of(k):
-        return pl.ds(0, half) if k == 0 else pl.ds(half + (k - 1) * (half // 2), half // 2)
+        return (pl.ds(0, half), pl.ds(half, half * 3 // 4), pl.ds(half + half * 3 // 4, half // 4))[k]
 
     def pieces_of(g):
         return (0,) if g == 0 else (1, 2)
@@ -320,6 +320,14 @@
     def _():
         to_across.wait()
 
+    @pl.when(place == 1)
+    def _():
+        hand_over(turn.at[4])
+
+    @pl.when(place == 0)
+    def _():
+        pl.semaphore_wait(turn.at[4], 1)
+
     for u in range(2):
         total = None
         for slot, reach in ((0, 4), (1, 2), (2, 6)):
@@ -582,7 +590,7 @@
 
     lax.fori_loop(0, 2, advance, 0)
 
-    @pl.when((core == 1) & jnp.logical_not(second_head))
+    @pl.when((core == 1) & jnp.logical_not(in_second))
     def _():
         wait_sent()
 
@@ -594,6 +602,11 @@
     @pl.when(in_second & (slab < last))
     def _():
         def use(u, carry):
+            @pl.when((core == 1) & jnp.logical_not(second_head))
+            def _():
+                for k in range(3):
+                    chain_copy(u, k).wait_send()
+
             @pl.when(jnp.logical_not(relays))
             def _():
                 for c in range(CHUNKS):
@@ -646,7 +659,7 @@
             dma((2, 3)),
             dma((2, 3)),
             pltpu.SemaphoreType.REGULAR((2,)),
-            pltpu.SemaphoreType.REGULAR((4,)),
+            pltpu.SemaphoreType.REGULAR((5,)),
         ],
         compiler_params=pltpu.CompilerParams(
             collective_id=0, has_side_effects=True, vmem_limit_bytes=60 * 1024 * 1024

time: 88.5 us -> 85.5 us (0.966)
  the two profiles are of different devices: /device:TPU:389 before, /device:TPU:489 now
where the time goes in v5:
time: 85.5 us; the launch traced here: 85.3 us
  Pallas kernels  84.4 us (99%)
  local copies, waits for them, and re-layouts  0.97 us (1%)
    pallas_call x1, Pallas kernels, body(): pl.pallas_call(kernel, out_shape=pltpu.VMEM(retarded.shape, F32), in_spec...  84.4 us

profile of v5, /device:TPU:489, one launch (start us, length us, event | category | flops | bytes accessed | tf_op | source)
XLA Modules:
  0.0 85.3 jit_solution(17236815582704187882)
XLA Ops:
  0.0 84.4 %shard_map.73 = f32[1,2,2,256,256]{4,3,2,1,0:T(8,128)S(1)} custom-call(f32[1,2,2,256,256]{4,3,2,1,0:T(8,128)} %retarded_hbm.1, f32[1,2,2,256,256]{4,3,2,1,0:T(8,128)} %lesser_hbm.1, f32[1,256,256]{2,1,0:T(8,128)} %hop_hbm.1, s32[1,4,4]{2,1,0:T(4,128)} %mask_ref.1, s32[3]{0:T(128)} %offsets_ref.1, f32[3]{0:T(128)} %coupling_ref.1, f32[3]{0:T(128)} %occupation_ref.1), custom_call_target="tpu_custom_call" | custom-call | tf_op jit(solution)/shard_map/pallas_call | solution.py:633
  84.4 1.0 %copy.9 = f32[1,2,2,256,256]{4,3,2,1,0:T(8,128)} copy(f32[1,2,2,256,256]{4,3,2,1,0:T(8,128)S(1)} %shard_map.73) | data formatting | bytes 2097152
